TPU v7x, 32 devices: a whole 2x2x4 slice. The times are simulated.
32 devices in a mesh: groups: 2 (over y), ep: 16 (over z, x, core).
Axes of the slice: x: 2, y: 2, z: 4, core: 2. Of those that a mesh axis runs over, the one named last changes fastest.
Arguments:
- hidden: bfloat16 [64, 7168], P(('groups', 'ep')), parts along dimension 0, may hold values from -6 to 6
- queries: bfloat16 [64, 128, 576], P(('groups', 'ep')), parts along dimension 0, may hold values from -40 to 40
- latent_cache: bfloat16 [64, 2048, 576], P(('groups', 'ep')), parts along dimension 0, may hold values from -8 to 8
- cache_lengths: int32 [64], P(('groups', 'ep')), parts along dimension 0, may hold values from 2 to 2048, as said below
- value_up: bfloat16 [128, 512, 128], P('ep'), may hold values from -0.25 to 0.25
- out_proj: bfloat16 [16384, 7168], P('ep'), may hold values from -0.046875 to 0.046875
- norm_gain: float32 [7168], replicated, may hold values from 0.1 to 1.9
- expert_ids: int32 [64, 8], P(('groups', 'ep')), parts along dimension 0, may hold values from 0 to 15, all different within a row; in each aligned block of 2 rows (0 to 1, 2 to 3, ...) at most 2 rows name the same one
- gate_weights: float32 [64, 8], P(('groups', 'ep')), parts along dimension 0, may hold values from 0.05 to 0.5
- gate_proj: bfloat16 [16, 7168, 1024], P('ep'), may hold values from -0.0625 to 0.0625
- up_proj: bfloat16 [16, 7168, 1024], P('ep'), may hold values from -0.0625 to 0.0625
- down_proj: bfloat16 [16, 1024, 7168], P('ep'), may hold values from -0.1875 to 0.1875
Outputs:
- layer_out: bfloat16 [64, 7168], P(('groups', 'ep')), parts along dimension 0
There are 2 independent parts, one for each index of `groups`. A program takes and returns all parts, laid end to end along the dimension named above; an argument that names none is the same for every part. Nothing has to cross between parts.
Inputs may be any that keep to these rules, and one draw needn't show every extreme that they name: `cache_lengths`: some row of each draw has exactly 2048 live positions and some row exactly 2. `expert_ids`: each row names 8 different experts. The 2 rows of one device name any one expert at most 2 times, so a device sends each expert at most 2 rows; some device of every draw reaches that.
All inputs are finite; a program needn't handle non-finite values.
Results may differ from a plain program's by a relative error of at most 0.0095.
Values may be sent and summed in bfloat16 or wider, within the bound.
A program may use at most 128 MiB of HBM per device.

v0:
```python
import jax
import jax.numpy as jnp
from jax import lax
from jax.sharding import PartitionSpec as P

EXPERTS = 16


score_scale = 0.07216878364870323
norm_eps = 1e-06


def partner(value, axis, bit):
    return lax.ppermute(value, axis, [(i, i ^ 1 << bit) for i in range(lax.axis_size(axis))])


def attend_and_project(hidden, queries, latent_cache, cache_lengths, value_up, out_proj):
    latent = value_up.shape[1]
    scores = (
        jnp.einsum("rhk,rtk->rht", queries, latent_cache, preferred_element_type=jnp.float32)
        * score_scale
    )
    positions = lax.broadcasted_iota(jnp.int32, scores.shape, 2)
    scores = jnp.where(positions < cache_lengths[:, None, None], scores, -jnp.inf)
    row_peak = jnp.max(scores, axis=2, keepdims=True)
    exp_scores = jnp.exp(scores - row_peak)
    soft_weights = (exp_scores / jnp.sum(exp_scores, axis=2, keepdims=True)).astype(jnp.bfloat16)
    latent_out = jnp.einsum(
        "rht,rtl->rhl",
        soft_weights,
        latent_cache[:, :, :latent],
        preferred_element_type=jnp.float32,
    ).astype(jnp.bfloat16)
    by_head = lax.all_to_all(latent_out, "ep", split_axis=1, concat_axis=0, tiled=True)
    head_out = jnp.einsum(
        "rhl,hlv->rhv", by_head, value_up, preferred_element_type=jnp.float32
    ).astype(jnp.bfloat16)
    head_rows = head_out.reshape(head_out.shape[0], head_out.shape[1] * head_out.shape[2])
    attention = lax.psum_scatter(
        jnp.dot(head_rows, out_proj, preferred_element_type=jnp.float32),
        "ep",
        scatter_dimension=0,
        tiled=True,
    )
    return hidden.astype(jnp.float32) + attention


def on_device(
    hidden,
    queries,
    latent_cache,
    cache_lengths,
    value_up,
    out_proj,
    norm_gain,
    expert_ids,
    gate_weights,
    gate_proj,
    up_proj,
    down_proj,
):
    rows_dev = hidden.shape[0]
    ep_size = lax.axis_size("ep")
    residual = attend_and_project(hidden, queries, latent_cache, cache_lengths, value_up, out_proj)
    inv_rms = lax.rsqrt(jnp.mean(residual * residual, axis=1, keepdims=True) + norm_eps)
    moe_in = (residual * inv_rms * norm_gain[None, :]).astype(jnp.bfloat16)
    split_ways = ep_size // EXPERTS
    slice_width = moe_in.shape[1] // split_ways
    experts_iota = lax.broadcasted_iota(jnp.int32, (1, 1, EXPERTS), 2)
    member = jnp.sum((expert_ids[:, :, None] == experts_iota).astype(jnp.int32), axis=1)
    before = jnp.cumsum(member, axis=0) - member
    slot_of = jnp.take_along_axis(before, expert_ids, axis=1)
    slot_iota = lax.broadcasted_iota(jnp.int32, (1, rows_dev, 1), 1)
    chosen = (member.T[:, None, :] == 1) & (before.T[:, None, :] == slot_iota)
    selection = chosen.astype(jnp.bfloat16)
    pieces = moe_in.reshape(rows_dev, split_ways, slice_width)
    outgoing = jnp.einsum(
        "ecr,rjd->jecd", selection, pieces, preferred_element_type=jnp.float32
    ).astype(jnp.bfloat16)
    outgoing = outgoing.reshape(ep_size, rows_dev, slice_width)
    incoming = lax.all_to_all(outgoing, "ep", split_axis=0, concat_axis=0, tiled=True)
    slot_rows = incoming.reshape(ep_size * rows_dev, slice_width)
    gate_act = jnp.dot(slot_rows, gate_proj[0], preferred_element_type=jnp.float32)
    up_act = jnp.dot(slot_rows, up_proj[0], preferred_element_type=jnp.float32)
    stacked = jnp.stack((gate_act, up_act))
    low_bit = EXPERTS.bit_length() - 1
    levels = split_ways.bit_length() - 1
    for swap_level in range(levels):
        stacked = stacked + partner(
            stacked.astype(jnp.bfloat16), "ep", low_bit + swap_level
        ).astype(stacked.dtype)
    hidden_units = (jax.nn.silu(stacked[0]) * stacked[1]).astype(jnp.bfloat16)
    expert_out = jnp.dot(hidden_units, down_proj[0], preferred_element_type=jnp.float32).astype(
        jnp.bfloat16
    )
    expert_out = expert_out.reshape(ep_size, rows_dev, slice_width)
    returned = lax.all_to_all(expert_out, "ep", split_axis=0, concat_axis=0, tiled=True)
    full_rows = returned.reshape(split_ways, EXPERTS, rows_dev, slice_width).transpose(1, 2, 0, 3)
    full_rows = full_rows.reshape(EXPERTS * rows_dev, split_ways * slice_width)
    picked = jnp.take(full_rows, expert_ids * rows_dev + slot_of, axis=0)
    routed_sum = jnp.sum(gate_weights[:, :, None] * picked.astype(jnp.float32), axis=1)
    return (residual + routed_sum).astype(jnp.bfloat16)


def solution(mesh):
    return jax.shard_map(
        on_device,
        mesh=mesh,
        in_specs=(
            P(("groups", "ep"), None),
            P(("groups", "ep"), None, None),
            P(("groups", "ep"), None, None),
            P(("groups", "ep")),
            P("ep", None, None),
            P("ep", None),
            P(),
            P(("groups", "ep"), None),
            P(("groups", "ep"), None),
            P("ep", None, None),
            P("ep", None, None),
            P("ep", None, None),
        ),
        out_specs=P(("groups", "ep"), None),
        check_vma=False,
    )
```

profile of v0, /device:TPU:0, one launch (start us, length us, event | category | flops | bytes accessed | tf_op | source)
XLA Modules:
  0.0 203.2 jit_solution(1262603272513919363)
XLA Ops:
  6.5 0.0 copy-start
  6.5 0.0 all-reduce.3.cloned.1.call-start
  6.5 3.6 %fusion.15 = f32[2,128,2048]{2,1,0:T(8,128)S(1)} fusion(bf16[2,128,576]{1,2,0:T(8,128)(2,1)} %param.13, bf16[2,2048,576]{1,2,0:T(8,128)(2,1)} %param.14, s32[2]{0:T(128)} %param.15), kind=kOutput, calls=%fused_computation.17 | convolution fusion | flops 605552640 | bytes 7110664 | tf_op jit(solution)/shard_map/rhk,rtk->rht/dot_general | solution.py:20
  10.1 0.5 fusion.47
  10.6 3.8 %fusion.16 = bf16[2,128,512]{2,1,0:T(8,128)(2,1)S(1)} fusion(bf16[2,2048,576]{1,2,0:T(8,128)(2,1)} %param.14, f32[2,128]{1,0:T(2,128)S(1)} %fusion.47, f32[2,128,2048]{2,1,0:T(8,128)S(1)} %fusion.15), kind=kOutput, calls=%fused_computation.20 | convolution fusion | flops 538577152 | bytes 8651776 | tf_op jit(solution)/shard_map/rht,rtl->rhl/dot_general | solution.py:28
  14.4 0.3 copy.25
  14.7 17.2 %all_to_all.28 = bf16[2,128,512]{2,0,1:T(2,128)(2,1)S(1)} all-to-all(bf16[2,128,512]{2,0,1:T(2,128)(2,1)S(1)} %copy.25), channel_id=1, replica_groups=mesh['groups'=2,'ep'=16] {'ep'}, dimensions={1} | all-to-all | bytes 524288 | tf_op jit(solution)/shard_map/all_to_all | solution.py:34
  31.9 0.2 copy.36
  32.1 0.1 all_to_all.22
  32.2 0.0 copy-done
  32.2 0.3 fusion.25
  32.5 0.0 copy-start.4
  32.5 0.0 copy-start.6
  32.5 0.0 copy-start.2
  32.5 0.0 copy-start.3
  32.5 8.8 %fusion.34 = f32[32,7168]{1,0:T(8,128)} fusion(bf16[1024,7168]{1,0:T(8,128)(2,1)} %param.17, bf16[8,4,8,128]{3,2,1,0:T(8,128)(2,1)S(1)} %fusion.25), kind=kOutput, calls=%fused_computation.34 | convolution fusion | flops 469762048 | bytes 15663104 | tf_op jit(solution)/shard_map/dot_general | solution.py:40
  41.3 0.0 all-reduce.3.cloned.1.call-update
  41.4 0.0 copy-done.4
  41.4 0.1 convert_reduce_fusion
  41.5 0.0 copy-done.6
  41.5 0.6 dynamic-slice
  42.8 89.3 %all-reduce.3.cloned.1.call-done = f32[32,7168]{1,0:T(8,128)} async-done(((f32[32,7168]{1,0:T(8,128)}), f32[32,7168]{1,0:T(8,128)}) %all-reduce.3.cloned.1.call-update) | async-done | bytes 917520
  132.1 0.0 copy-done.2
  132.1 1.1 multiply_reduce_fusion.1
  133.2 0.0 copy-done.3
  133.2 1.3 fusion.10
  134.5 0.5 copy.28
  135.0 18.0 %all_to_all.29 = bf16[16,2,7168]{2,1,0:T(2,128)(2,1)S(1)} all-to-all(bf16[16,2,7168]{2,1,0:T(2,128)(2,1)S(1)} %copy.28), channel_id=1, replica_groups=mesh['groups'=2,'ep'=16] {'ep'}, dimensions={0} | all-to-all | bytes 917504 | tf_op jit(solution)/shard_map/all_to_all | solution.py:81
  152.9 0.2 reshape.51
  153.1 7.8 %fusion.5 = f32[32,1024]{1,0:T(8,128)S(1)} fusion(bf16[32,7168]{1,0:T(8,128)(2,1)S(1)} %reshape.51, bf16[1,7168,1024]{2,1,0:T(8,128)(2,1)} %param.21), kind=kOutput, calls=%fused_computation.7 | convolution fusion | flops 469762048 | bytes 15269888 | tf_op jit(solution)/shard_map/dot_general | solution.py:83
  160.9 0.0 copy-start.1
  160.9 14.6 %fusion.7 = bf16[32,7168]{1,0:T(8,128)(2,1)S(1)} fusion(bf16[1,1024,7168]{2,1,0:T(8,128)(2,1)} %param.23, bf16[32,7168]{1,0:T(8,128)(2,1)S(1)} %reshape.51, bf16[1,7168,1024]{2,1,0:T(8,128)(2,1)} %param.22, f32[32,1024]{1,0:T(8,128)S(1)} %fusion.5), kind=kOutput, calls=%fused_computation.9 | convolution fusion | flops 939950080 | bytes 30408704 | tf_op jit(solution)/shard_map/dot_general | solution.py:93
  175.6 0.0 copy-start.5
  175.6 1.0 reshape.52
  176.6 3.8 %all-to-all-start.2 = ((bf16[16,2,7168]{2,1,0:T(2,128)(2,1)}), bf16[16,2,7168]{2,1,0:T(2,128)(2,1)S(1)}, u32[]{:S(2)}, u32[]{:S(2)}) async-start(bf16[16,2,7168]{2,1,0:T(2,128)(2,1)} %reshape.52), calls=%async_computation.2 | async-start | bytes 917504 | tf_op jit(solution)/shard_map/all_to_all | solution.py:97
  180.4 0.1 reshape.61
  180.5 0.7 gather_fusion.1
  181.1 0.1 reshape.64
  181.2 0.1 reshape.55
  181.3 12.2 %all-to-all-done.2 = bf16[16,2,7168]{2,1,0:T(2,128)(2,1)S(1)} async-done(((bf16[16,2,7168]{2,1,0:T(2,128)(2,1)}), bf16[16,2,7168]{2,1,0:T(2,128)(2,1)S(1)}, u32[]{:S(2)}, u32[]{:S(2)}) %all-to-all-start.2) | async-done | bytes 458784 | tf_op jit(solution)/shard_map/all_to_all | solution.py:97
  193.6 0.2 reshape_transpose_reshape.3
  193.8 0.7 gather_fusion
  194.4 0.0 copy-done.5
  194.5 0.3 multiply_reduce_fusion
  194.7 1.6 add_convert_fusion
  196.3 0.0 copy-done.1
  (7 shorter events, 0.1 us)
Async XLA Ops:
  6.5 25.6 %copy-start = (bf16[8,512,128]{2,1,0:T(8,128)(2,1)S(1)}, bf16[8,512,128]{2,1,0:T(8,128)(2,1)}, u32[]{:S(2)}) copy-start(bf16[8,512,128]{2,1,0:T(8,128)(2,1)} %param.16) | copy-start | bytes 3145732
  6.5 125.5 %all-reduce.3.cloned.1.call-start = ((), (), s32[]{:S(2)}) async-start(), calls=%async_computation.3 | async-start | bytes 1835008
  32.5 8.9 %copy-start.4 = (s32[2,8]{1,0:T(2,128)S(1)}, s32[2,8]{1,0:T(2,128)}, u32[]{:S(2)}) copy-start(s32[2,8]{1,0:T(2,128)} %param.19) | copy-start | bytes 196
  32.5 9.1 %copy-start.6 = (u32[32]{0:T(128)S(1)}, u32[32]{0:T(128)}, u32[]{:S(2)}) copy-start(u32[32]{0:T(128)} %constant.78) | copy-start | bytes 388
  32.5 99.6 %copy-start.2 = (bf16[2,7168]{1,0:T(2,128)(2,1)S(1)}, bf16[2,7168]{1,0:T(2,128)(2,1)}, u32[]{:S(2)}) copy-start(bf16[2,7168]{1,0:T(2,128)(2,1)} %param.12) | copy-start | bytes 86020
  32.5 100.7 %copy-start.3 = (f32[7168]{0:T(1024)S(1)}, f32[7168]{0:T(1024)}, u32[]{:S(2)}) copy-start(f32[7168]{0:T(1024)} %param.18) | copy-start | bytes 86020
  160.9 35.4 %copy-start.1 = (bf16[8,512,128]{2,1,0:T(8,128)(2,1)S(1)}, bf16[8,512,128]{2,1,0:T(8,128)(2,1)}, u32[]{:S(2)}) copy-start(bf16[8,512,128]{2,1,0:T(8,128)(2,1)} %param.16) | copy-start | bytes 3145732
  175.6 18.9 %copy-start.5 = (f32[2,8]{1,0:T(2,128)S(1)}, f32[2,8]{1,0:T(2,128)}, u32[]{:S(2)}) copy-start(f32[2,8]{1,0:T(2,128)} %param.20) | copy-start | bytes 196
  176.6 17.0 %all-to-all-start.2 = ((bf16[16,2,7168]{2,1,0:T(2,128)(2,1)}), bf16[16,2,7168]{2,1,0:T(2,128)(2,1)S(1)}, u32[]{:S(2)}, u32[]{:S(2)}) async-start(bf16[16,2,7168]{2,1,0:T(2,128)(2,1)} %reshape.52), calls=%async_computation.2 | async-start | bytes 917504 | tf_op jit(solution)/shard_map/all_to_all | solution.py:97
Sparse Core Ops, SparseCore 0:
  41.5 90.5 all-reduce.2
where the time goes:
time: 204 us; the launch traced here: 203 us
  waiting for transfers between devices  102 us (50%)
  matrix products  40.2 us (20%)
  blocking collectives  35.2 us (17%)
  between operations  14.2 us (7%)
  local copies, waits for them, and re-layouts  4.57 us (2%)
  starting transfers between devices  3.8 us (2%)
  other arithmetic  3.63 us (2%)
    unnamed x2, waiting for transfers between devices  89.3 us
    all_to_all x1, blocking collectives, on_device(): lax.all_to_all(outgoing, 'ep', split_axis=0, concat_axis=0, tiled=True)  18 us
    all_to_all x1, blocking collectives, attend_and_project(): lax.all_to_all(latent_out, 'ep', split_axis=1, concat_axis=0, tiled=True)  17.2 us
    dot_general x1, matrix products, on_device(): jnp.dot(hidden_units, down_proj[0], preferred_element_type=jnp.float32)  14.6 us
    all_to_all x1, waiting for transfers between devices, on_device(): lax.all_to_all(expert_out, 'ep', split_axis=0, concat_axis=0, tiled=True)  12.2 us
    dot_general x1, matrix products, attend_and_project(): jnp.dot(head_rows, out_proj, preferred_element_type=jnp.float32)  8.84 us
    dot_general x1, matrix products, on_device(): jnp.dot(slot_rows, gate_proj[0], preferred_element_type=jnp.float32)  7.81 us
  transfers between devices with their start and end apart: 2, of which 2 were waited for; matrix products, arithmetic and copies ran while one was open for 1% of the time, Pallas kernels for 0%

commit v1 on v0

--- a/solution.py
+++ b/solution.py
@@ -1,6 +1,10 @@
+import functools
+
 import jax
 import jax.numpy as jnp
 from jax import lax
+from jax.experimental import pallas as pl
+from jax.experimental.pallas import tpu as pltpu
 from jax.sharding import PartitionSpec as P
 
 EXPERTS = 16
@@ -102,9 +106,498 @@
     return (residual + routed_sum).astype(jnp.bfloat16)
 
 
+PLANE = 4
+CHUNKS = 4
+TILE = 256
+
+
+def remote(src, dst, send_sem, recv_sem, peer):
+    return pltpu.make_async_remote_copy(
+        src_ref=src,
+        dst_ref=dst,
+        send_sem=send_sem,
+        recv_sem=recv_sem,
+        device_id={"ep": peer},
+        device_id_type=pl.DeviceIdType.MESH,
+    )
+
+
+def fused_kernel(
+    n,
+    hidden,
+    queries,
+    cache,
+    lengths,
+    value_up,
+    out_proj,
+    gain,
+    ids,
+    weights,
+    gate_proj,
+    up_proj,
+    down_proj,
+    out,
+    q_buf,
+    c_buf,
+    vu_buf,
+    w_buf,
+    g_buf,
+    u_buf,
+    lat_send,
+    lat_recv,
+    lat_f32,
+    heads,
+    part_f32,
+    a_send,
+    a_recv,
+    b_f32,
+    b_send,
+    b_recv,
+    residual,
+    own_rows,
+    z_recv,
+    p_f32,
+    p_send,
+    p_recv,
+    info_own,
+    info_all,
+    info_rows,
+    g_acc,
+    u_acc,
+    units,
+    load_sem,
+    w_sem,
+    gu_sem,
+    d_sem,
+    lat_ss,
+    lat_rs,
+    a_ss,
+    a_rs,
+    b_ss,
+    b_rs,
+    z_ss,
+    z_rs,
+    p_ss,
+    p_rs,
+    i_ss,
+    i_rs,
+):
+    me = lax.axis_index("ep")
+    planes = n // PLANE
+    my_q = lax.rem(me, PLANE)
+    my_z = lax.div(me, PLANE)
+    rows_dev, n_heads, _ = q_buf.shape
+    heads_dev, latent, vdim = vu_buf.shape
+    width = hidden.shape[1]
+    cc = width // CHUNKS
+    ctx = c_buf.shape[1]
+    rows = n * rows_dev
+    prows = planes * rows_dev
+    bf16, f32 = jnp.bfloat16, jnp.float32
+
+    def plane_peer(k):
+        return my_z * PLANE + lax.rem(my_q + k, PLANE)
+
+    def z_peer(k):
+        return lax.rem(my_z + k, planes) * PLANE + my_q
+
+    loads = [pltpu.make_async_copy(queries, q_buf, load_sem.at[0])]
+    for r in range(rows_dev):
+        loads.append(pltpu.make_async_copy(cache.at[r], c_buf.at[r], load_sem.at[1 + r]))
+    load_vu = pltpu.make_async_copy(value_up, vu_buf, load_sem.at[1 + rows_dev])
+    for copy in loads:
+        copy.start()
+    load_vu.start()
+
+    barrier = pltpu.get_barrier_semaphore()
+
+    @pl.loop(1, n)
+    def _(k):
+        pl.semaphore_signal(
+            barrier,
+            inc=1,
+            device_id={"ep": lax.rem(me + k, n)},
+            device_id_type=pl.DeviceIdType.MESH,
+        )
+
+    kd = w_buf.shape[0] // CHUNKS
+
+    def w_copy(src, sem, i):
+        span = pl.ds(i * kd, kd)
+        return pltpu.make_async_copy(src.at[span, :], w_buf.at[span, :], sem.at[i])
+
+    def gu_copy(src, dst, j, i):
+        span = pl.ds(i * cc, cc)
+        return pltpu.make_async_copy(src.at[0, span, :], dst.at[span, :], gu_sem.at[j, i])
+
+    loads[0].wait()
+    for r in range(rows_dev):
+        loads[1 + r].wait()
+        if r == rows_dev - 1:
+            for i in range(CHUNKS):
+                w_copy(out_proj, w_sem, i).start()
+            for i in range(CHUNKS):
+                gu_copy(gate_proj, g_buf, 0, i).start()
+                gu_copy(up_proj, u_buf, 1, i).start()
+        scores = (
+            lax.dot_general(
+                q_buf[r], c_buf[r], (((1,), (1,)), ((), ())), preferred_element_type=f32
+            )
+            * score_scale
+        )
+        positions = lax.broadcasted_iota(jnp.int32, scores.shape, 1)
+        scores = jnp.where(positions < lengths[r], scores, -jnp.inf)
+        peak = jnp.max(scores, axis=1, keepdims=True)
+        expd = jnp.exp(scores - peak)
+        total = jnp.sum(expd, axis=1, keepdims=True)
+        acc = jnp.dot(expd.astype(bf16), c_buf[r, :, :latent], preferred_element_type=f32)
+        acc = acc / total
+        for d in range(n):
+            lat_send[r, d] = acc[d * heads_dev : (d + 1) * heads_dev].astype(bf16)
+        if r == 0:
+            pl.semaphore_wait(barrier, n - 1)
+        slot = my_q * prows + my_z * rows_dev + r
+
+        @pl.loop(1, n)
+        def _(k):
+            peer = lax.rem(me + k, n)
+            remote(
+                lat_send.at[r, peer], lat_recv.at[slot], lat_ss.at[r, k], lat_rs.at[r, k], peer
+            ).start()
+
+        lat_recv[slot] = lat_send[r, me]
+
+    lane = lax.broadcasted_iota(jnp.int32, (rows_dev, 128), 1)
+    info = jnp.zeros((rows_dev, 128), f32)
+    for k in range(ids.shape[1]):
+        info = info + jnp.where(lane == ids[:, k : k + 1], weights[:, k : k + 1], 0.0)
+
+    load_vu.wait()
+    for r in range(rows_dev):
+
+        @pl.loop(1, n)
+        def _(k):
+            peer = lax.rem(me + n - k, n)
+            slot = lax.rem(peer, PLANE) * prows + lax.div(peer, PLANE) * rows_dev + r
+            remote(
+                lat_send.at[r, peer], lat_recv.at[slot], lat_ss.at[r, k], lat_rs.at[r, k], peer
+            ).wait_recv()
+
+    for i in range(rows):
+        block = lat_recv[i].astype(f32)
+        for j in range(latent // 128):
+            lat_f32[j, i * heads_dev : (i + 1) * heads_dev, :] = block[:, j * 128 : (j + 1) * 128]
+    for h in range(heads_dev):
+        lhs = jnp.concatenate(
+            [lat_f32[j, pl.ds(h, rows, stride=heads_dev), :] for j in range(latent // 128)], axis=1
+        ).astype(bf16)
+        heads[:, h * vdim : (h + 1) * vdim] = jnp.dot(
+            lhs, vu_buf[h], preferred_element_type=f32
+        ).astype(bf16)
+
+    def stage_a(which, c, lhs, row_scale):
+        @pl.loop(0, cc // TILE)
+        def _(t):
+            inner = pl.ds(pl.multiple_of(t * TILE, TILE), TILE)
+            cols = pl.ds(pl.multiple_of(c * cc + t * TILE, TILE), TILE)
+            part = jnp.dot(lhs[...], w_buf[:, cols], preferred_element_type=f32)
+            if row_scale is not None:
+                part = part * row_scale
+            for q in range(PLANE):
+                piece = part[q * prows : (q + 1) * prows]
+                part_f32[c, q, :, inner] = piece
+                a_send[which, c, q, :, inner] = piece.astype(bf16)
+
+        for k in range(1, PLANE):
+            a_copy(which, c, k).start()
+
+    def a_copy(which, c, k):
+        return remote(
+            a_send.at[which, c, lax.rem(my_q + k, PLANE)],
+            a_recv.at[which, c, k - 1],
+            a_ss.at[which, c, k - 1],
+            a_rs.at[which, c, k - 1],
+            plane_peer(k),
+        )
+
+    def stage_b(which, c):
+        total = part_f32[c, my_q]
+        for k in range(1, PLANE):
+            a_copy(which, c, k).wait_recv()
+            total = total + a_recv[which, c, k - 1].astype(f32)
+        for z in range(planes):
+            piece = total[z * rows_dev : (z + 1) * rows_dev]
+            b_f32[c, z] = piece
+            b_send[which, c, z] = piece.astype(bf16)
+        for k in range(1, planes):
+            b_copy(which, c, k).start()
+
+    def b_copy(which, c, k):
+        return remote(
+            b_send.at[which, c, lax.rem(my_z + k, planes)],
+            b_recv.at[which, c, k - 1],
+            b_ss.at[which, c, k - 1],
+            b_rs.at[which, c, k - 1],
+            z_peer(k),
+        )
+
+    def stage_sum(which, c):
+        total = b_f32[c, my_z]
+        for k in range(1, planes):
+            b_copy(which, c, k).wait_recv()
+            total = total + b_recv[which, c, k - 1].astype(f32)
+        return total
+
+    def z_copy(c, k):
+        return remote(
+            own_rows.at[c], z_recv.at[c, my_z], z_ss.at[c, k - 1], z_rs.at[c, k - 1], z_peer(k)
+        )
+
+    def z_arrival(c, k):
+        return remote(
+            own_rows.at[c],
+            z_recv.at[c, lax.rem(my_z + planes - k, planes)],
+            z_ss.at[c, k - 1],
+            z_rs.at[c, k - 1],
+            z_peer(k),
+        )
+
+    def p_copy(c, k):
+        return remote(
+            p_send.at[c], p_recv.at[c, my_q], p_ss.at[c, k - 1], p_rs.at[c, k - 1], plane_peer(k)
+        )
+
+    def p_arrival(c, k):
+        return remote(
+            p_send.at[c],
+            p_recv.at[c, lax.rem(my_q + PLANE - k, PLANE)],
+            p_ss.at[c, k - 1],
+            p_rs.at[c, k - 1],
+            plane_peer(k),
+        )
+
+    for i in range(CHUNKS):
+        w_copy(out_proj, w_sem, i).wait()
+    for c in range(CHUNKS):
+        stage_a(0, c, heads, None)
+    for i in range(CHUNKS):
+        w_copy(down_proj.at[0], d_sem, i).start()
+    for c in range(CHUNKS):
+        stage_b(0, c)
+    square = jnp.zeros((rows_dev, 1), f32)
+    for c in range(CHUNKS):
+        cols = slice(c * cc, (c + 1) * cc)
+        value = hidden[:, cols].astype(f32) + stage_sum(0, c)
+        residual[c] = value
+        square = square + jnp.sum(value * value, axis=1, keepdims=True)
+        scaled = (value * gain[:, cols]).astype(bf16)
+        own_rows[c] = scaled
+        for k in range(1, planes):
+            z_copy(c, k).start()
+        z_recv[c, my_z] = scaled
+    inv_rms = lax.rsqrt(square * (1.0 / width) + norm_eps)
+    info_own[...] = jnp.where(lane == 127, inv_rms, info)
+    my_slot = my_q * planes + my_z
+
+    @pl.loop(1, n)
+    def _(k):
+        remote(
+            info_own, info_all.at[my_slot], i_ss.at[k], i_rs.at[k], lax.rem(me + k, n)
+        ).start()
+
+    info_all[my_slot] = info_own[...]
+    for c in range(CHUNKS):
+        for k in range(1, planes):
+            z_arrival(c, k).wait_recv()
+        for z in range(planes):
+            p_f32[c, z * rows_dev : (z + 1) * rows_dev, :] = z_recv[c, z].astype(f32)
+        block = p_f32[c].astype(bf16)
+        p_send[c] = block
+        for k in range(1, PLANE):
+            p_copy(c, k).start()
+        p_recv[c, my_q] = block
+
+    for c in range(CHUNKS):
+        gu_copy(gate_proj, g_buf, 0, c).wait()
+        gu_copy(up_proj, u_buf, 1, c).wait()
+        for k in range(1, PLANE):
+            p_arrival(c, k).wait_recv()
+        x = jnp.concatenate([p_recv[c, q].astype(f32) for q in range(PLANE)], axis=0).astype(bf16)
+
+        @pl.loop(0, g_acc.shape[1] // TILE)
+        def _(t):
+            cols = pl.ds(pl.multiple_of(t * TILE, TILE), TILE)
+            span = slice(c * cc, (c + 1) * cc)
+            g = jnp.dot(x, g_buf[span, cols], preferred_element_type=f32)
+            u = jnp.dot(x, u_buf[span, cols], preferred_element_type=f32)
+            if c > 0:
+                g = g + g_acc[:, cols]
+                u = u + u_acc[:, cols]
+            g_acc[:, cols] = g
+            u_acc[:, cols] = u
+
+    @pl.loop(1, n)
+    def _(k):
+        peer = lax.rem(me + n - k, n)
+        slot = lax.rem(peer, PLANE) * planes + lax.div(peer, PLANE)
+        remote(info_own, info_all.at[slot], i_ss.at[k], i_rs.at[k], peer).wait_recv()
+
+    for i in range(n):
+        info_rows[i * rows_dev : (i + 1) * rows_dev, :] = info_all[i]
+    info = info_rows[...]
+    lane = lax.broadcasted_iota(jnp.int32, info.shape, 1)
+    row_inv = info[:, 127:128]
+    row_weight = jnp.sum(jnp.where(lane == me, info, 0.0), axis=1, keepdims=True)
+    gate = g_acc[...] * row_inv
+    units[...] = (gate / (1.0 + jnp.exp(-gate)) * (u_acc[...] * row_inv)).astype(bf16)
+    for i in range(CHUNKS):
+        w_copy(down_proj.at[0], d_sem, i).wait()
+    for c in range(CHUNKS):
+        stage_a(1, c, units, row_weight)
+    for c in range(CHUNKS):
+        stage_b(1, c)
+    for c in range(CHUNKS):
+        out[:, c * cc : (c + 1) * cc] = (residual[c] + stage_sum(1, c)).astype(bf16)
+
+    for r in range(rows_dev):
+
+        @pl.loop(1, n)
+        def _(k):
+            peer = lax.rem(me + k, n)
+            remote(
+                lat_send.at[r, peer], lat_recv.at[0], lat_ss.at[r, k], lat_rs.at[r, k], peer
+            ).wait_send()
+
+    @pl.loop(1, n)
+    def _(k):
+        remote(
+            info_own, info_all.at[0], i_ss.at[k], i_rs.at[k], lax.rem(me + k, n)
+        ).wait_send()
+
+    for c in range(CHUNKS):
+        for which in range(2):
+            for k in range(1, PLANE):
+                a_copy(which, c, k).wait_send()
+            for k in range(1, planes):
+                b_copy(which, c, k).wait_send()
+        for k in range(1, planes):
+            z_copy(c, k).wait_send()
+        for k in range(1, PLANE):
+            p_copy(c, k).wait_send()
+
+
+def fused_on_device(
+    hidden,
+    queries,
+    latent_cache,
+    cache_lengths,
+    value_up,
+    out_proj,
+    norm_gain,
+    expert_ids,
+    gate_weights,
+    gate_proj,
+    up_proj,
+    down_proj,
+):
+    n = lax.axis_size("ep")
+    planes = n // PLANE
+    rows_dev, width = hidden.shape
+    rows, prows = n * rows_dev, planes * rows_dev
+    heads_dev, latent, vdim = value_up.shape
+    ff = gate_proj.shape[2]
+    cc = width // CHUNKS
+    bf16, f32 = jnp.bfloat16, jnp.float32
+    vmem, anyspace = pl.BlockSpec(memory_space=pltpu.VMEM), pl.BlockSpec(memory_space=pl.ANY)
+    dma = pltpu.SemaphoreType.DMA
+    return pl.pallas_call(
+        functools.partial(fused_kernel, n),
+        out_shape=jax.ShapeDtypeStruct(hidden.shape, bf16),
+        in_specs=[
+            vmem,
+            anyspace,
+            anyspace,
+            pl.BlockSpec(memory_space=pltpu.SMEM),
+            anyspace,
+            anyspace,
+            vmem,
+            vmem,
+            vmem,
+            anyspace,
+            anyspace,
+            anyspace,
+        ],
+        out_specs=vmem,
+        scratch_shapes=[
+            pltpu.VMEM(queries.shape, bf16),
+            pltpu.VMEM(latent_cache.shape, bf16),
+            pltpu.VMEM(value_up.shape, bf16),
+            pltpu.VMEM(out_proj.shape, bf16),
+            pltpu.VMEM(gate_proj.shape[1:], bf16),
+            pltpu.VMEM(up_proj.shape[1:], bf16),
+            pltpu.VMEM((rows_dev, n, heads_dev, latent), bf16),
+            pltpu.VMEM((rows, heads_dev, latent), bf16),
+            pltpu.VMEM((latent // 128, rows * heads_dev, 128), f32),
+            pltpu.VMEM((rows, heads_dev * vdim), bf16),
+            pltpu.VMEM((CHUNKS, PLANE, prows, cc), f32),
+            pltpu.VMEM((2, CHUNKS, PLANE, prows, cc), bf16),
+            pltpu.VMEM((2, CHUNKS, PLANE - 1, prows, cc), bf16),
+            pltpu.VMEM((CHUNKS, planes, rows_dev, cc), f32),
+            pltpu.VMEM((2, CHUNKS, planes, rows_dev, cc), bf16),
+            pltpu.VMEM((2, CHUNKS, planes - 1, rows_dev, cc), bf16),
+            pltpu.VMEM((CHUNKS, rows_dev, cc), f32),
+            pltpu.VMEM((CHUNKS, rows_dev, cc), bf16),
+            pltpu.VMEM((CHUNKS, planes, rows_dev, cc), bf16),
+            pltpu.VMEM((CHUNKS, prows, cc), f32),
+            pltpu.VMEM((CHUNKS, prows, cc), bf16),
+            pltpu.VMEM((CHUNKS, PLANE, prows, cc), bf16),
+            pltpu.VMEM((rows_dev, 128), f32),
+            pltpu.VMEM((n, rows_dev, 128), f32),
+            pltpu.VMEM((rows, 128), f32),
+            pltpu.VMEM((rows, ff), f32),
+            pltpu.VMEM((rows, ff), f32),
+            pltpu.VMEM((rows, ff), bf16),
+            dma((2 + rows_dev,)),
+            dma((CHUNKS,)),
+            dma((2, CHUNKS)),
+            dma((CHUNKS,)),
+            dma((rows_dev, n)),
+            dma((rows_dev, n)),
+            dma((2, CHUNKS, PLANE - 1)),
+            dma((2, CHUNKS, PLANE - 1)),
+            dma((2, CHUNKS, planes - 1)),
+            dma((2, CHUNKS, planes - 1)),
+            dma((CHUNKS, planes - 1)),
+            dma((CHUNKS, planes - 1)),
+            dma((CHUNKS, PLANE - 1)),
+            dma((CHUNKS, PLANE - 1)),
+            dma((n,)),
+            dma((n,)),
+        ],
+        compiler_params=pltpu.CompilerParams(
+            collective_id=0, has_side_effects=True, vmem_limit_bytes=67043328
+        ),
+        name="fused_layer",
+    )(
+        hidden,
+        queries,
+        latent_cache,
+        cache_lengths,
+        value_up,
+        out_proj,
+        norm_gain[None, :],
+        expert_ids,
+        gate_weights,
+        gate_proj,
+        up_proj,
+        down_proj,
+    )
+
+
 def solution(mesh):
+    body = fused_on_device if mesh.shape["ep"] == EXPERTS else on_device
     return jax.shard_map(
-        on_device,
+        body,
         mesh=mesh,
         in_specs=(
             P(("groups", "ep"), None),

time: 204 us -> 71.2 us (0.35)
  waiting for transfers between devices: 102 us -> 0 us
  Pallas kernels: 0 us -> 59.8 us
  matrix products: 40.2 us -> 0 us
  blocking collectives: 35.2 us -> 0 us
  between operations: 14.2 us -> 0.01 us
  local copies, waits for them, and re-layouts: 4.57 us -> 10.9 us
  starting transfers between devices: 3.8 us -> 0 us
  other arithmetic: 3.63 us -> 0 us
    unnamed x2 -> x0, waiting for transfers between devices: 89.3 us -> none
    pallas_call x0 -> x1, Pallas kernels: none -> 59.8 us  [fused_on_device(): pl.pallas_call(functools.partial(fused_kernel, n), out_shape=jax.ShapeDty...]
    dot_general x7 -> x0, matrix products: 40.2 us -> none  [the longest x1 14.6 us: on_device(): jnp.dot(hidden_units, down_proj[0], preferred_element_type=jnp.float32)]
    all_to_all x2 -> x0, blocking collectives: 35.2 us -> none  [the longest x1 18 us: on_device(): lax.all_to_all(outgoing, 'ep', split_axis=0, concat_axis=0, tiled=True)]
    all_to_all x1 -> x0, waiting for transfers between devices: 12.2 us -> none  [on_device(): lax.all_to_all(expert_out, 'ep', split_axis=0, concat_axis=0, tiled=True)]
    unnamed x15 -> x3, local copies, waits for them, and re-layouts: 0.62 us -> 10.9 us
    all_to_all x1 -> x0, starting transfers between devices: 3.8 us -> none  [on_device(): lax.all_to_all(expert_out, 'ep', split_axis=0, concat_axis=0, tiled=True)]
  transfers between devices with their start and end apart: 2 -> 0, of which waited for: 2 -> 0; matrix products, arithmetic and copies ran while one was open for 1% -> 0% of each run, Pallas kernels for 0% -> 0%
where the time goes in v1:
time: 71.2 us; the launch traced here: 70.8 us
  Pallas kernels  59.8 us (84%)
  local copies, waits for them, and re-layouts  10.9 us (15%)
    pallas_call x1, Pallas kernels, fused_on_device(): pl.pallas_call(functools.partial(fused_kernel, n), out_shape=jax.ShapeDty...  59.8 us
    unnamed x3, local copies, waits for them, and re-layouts  10.9 us

profile of v1, /device:TPU:0, one launch (start us, length us, event | category | flops | bytes accessed | tf_op | source)
XLA Modules:
  0.0 70.8 jit_solution(16632104454742414072)
XLA Ops:
  0.0 1.9 %copy.13.queries = bf16[2,128,576]{2,1,0:T(8,128)(2,1)} copy(bf16[2,128,576]{1,2,0:T(8,128)(2,1)} %param.13) | data formatting | bytes 589824 | tf_op args[1]
  1.9 7.7 %copy.14.cache = bf16[2,2048,576]{2,1,0:T(8,128)(2,1)} copy(bf16[2,2048,576]{1,2,0:T(8,128)(2,1)} %param.14) | data formatting | bytes 9437184 | tf_op args[2]
  9.6 59.8 %fused_layer.1 = bf16[2,7168]{1,0:T(2,128)(2,1)} custom-call(bf16[2,7168]{1,0:T(2,128)(2,1)} %hidden.1, bf16[2,128,576]{2,1,0:T(8,128)(2,1)} %copy.13.queries, bf16[2,2048,576]{2,1,0:T(8,128)(2,1)} %copy.14.cache, s32[2]{0:T(128)} %lengths.1, bf16[8,512,128]{2,1,0:T(8,128)(2,1)} %value_up.1, bf16[1024,7168]{1,0:T(8,128)(2,1)} %out_proj.1, ...), custom_call_target="tpu_custom_call" | custom-call | tf_op jit(solution)/shard_map/fused_layer/pallas_call | solution.py:513
  69.4 1.4 %copy.16 = bf16[2,7168]{1,0:T(2,128)(2,1)} copy(bf16[2,7168]{1,0:T(2,128)(2,1)} %fused_layer.1) | data formatting | bytes 57344

commit v2 on v1

--- a/solution.py
+++ b/solution.py
@@ -107,8 +107,19 @@
 
 
 PLANE = 4
-CHUNKS = 4
-TILE = 256
+LOADS = 4
+
+
+def chunks_of(width):
+    return next(m for m in (7, 8, 4, 2, 1) if width % (m * 128) == 0)
+
+
+def step_order(chunks, spans):
+    ready = [(c * spans[0], 0, c) for c in range(chunks)]
+    for stage in range(1, len(spans)):
+        delay = sum(spans[1 : stage + 1])
+        ready += [((c + 1) * spans[0] + delay, stage, c) for c in range(chunks)]
+    return [(stage, c) for _, stage, c in sorted(ready)]
 
 
 def remote(src, dst, send_sem, recv_sem, peer):
@@ -186,11 +197,11 @@
     planes = n // PLANE
     my_q = lax.rem(me, PLANE)
     my_z = lax.div(me, PLANE)
-    rows_dev, n_heads, _ = q_buf.shape
+    rows_dev = q_buf.shape[0]
     heads_dev, latent, vdim = vu_buf.shape
     width = hidden.shape[1]
-    cc = width // CHUNKS
-    ctx = c_buf.shape[1]
+    chunks = chunks_of(width)
+    cc = width // chunks
     rows = n * rows_dev
     prows = planes * rows_dev
     bf16, f32 = jnp.bfloat16, jnp.float32
@@ -220,7 +231,7 @@
             device_id_type=pl.DeviceIdType.MESH,
         )
 
-    kd = w_buf.shape[0] // CHUNKS
+    kd = w_buf.shape[0] // LOADS
 
     def w_copy(src, sem, i):
         span = pl.ds(i * kd, kd)
@@ -233,15 +244,12 @@
     loads[0].wait()
     for r in range(rows_dev):
         loads[1 + r].wait()
-        if r == rows_dev - 1:
-            for i in range(CHUNKS):
+        if r == 0:
+            for i in range(LOADS):
                 w_copy(out_proj, w_sem, i).start()
-            for i in range(CHUNKS):
-                gu_copy(gate_proj, g_buf, 0, i).start()
-                gu_copy(up_proj, u_buf, 1, i).start()
         scores = (
             lax.dot_general(
-                q_buf[r], c_buf[r], (((1,), (1,)), ((), ())), preferred_element_type=f32
+                q_buf[r], c_buf[r], (((0,), (0,)), ((), ())), preferred_element_type=f32
             )
             * score_scale
         )
@@ -250,7 +258,12 @@
         peak = jnp.max(scores, axis=1, keepdims=True)
         expd = jnp.exp(scores - peak)
         total = jnp.sum(expd, axis=1, keepdims=True)
-        acc = jnp.dot(expd.astype(bf16), c_buf[r, :, :latent], preferred_element_type=f32)
+        acc = lax.dot_general(
+            expd.astype(bf16),
+            c_buf[r, :latent],
+            (((1,), (1,)), ((), ())),
+            preferred_element_type=f32,
+        )
         acc = acc / total
         for d in range(n):
             lat_send[r, d] = acc[d * heads_dev : (d + 1) * heads_dev].astype(bf16)
@@ -272,6 +285,9 @@
     for k in range(ids.shape[1]):
         info = info + jnp.where(lane == ids[:, k : k + 1], weights[:, k : k + 1], 0.0)
 
+    for i in range(chunks):
+        gu_copy(gate_proj, g_buf, 0, i).start()
+        gu_copy(up_proj, u_buf, 1, i).start()
     load_vu.wait()
     for r in range(rows_dev):
 
@@ -296,18 +312,14 @@
         ).astype(bf16)
 
     def stage_a(which, c, lhs, row_scale):
-        @pl.loop(0, cc // TILE)
-        def _(t):
-            inner = pl.ds(pl.multiple_of(t * TILE, TILE), TILE)
-            cols = pl.ds(pl.multiple_of(c * cc + t * TILE, TILE), TILE)
-            part = jnp.dot(lhs[...], w_buf[:, cols], preferred_element_type=f32)
-            if row_scale is not None:
-                part = part * row_scale
-            for q in range(PLANE):
-                piece = part[q * prows : (q + 1) * prows]
-                part_f32[c, q, :, inner] = piece
-                a_send[which, c, q, :, inner] = piece.astype(bf16)
-
+        cols = slice(c * cc, (c + 1) * cc)
+        part = jnp.dot(lhs[...], w_buf[:, cols], preferred_element_type=f32)
+        if row_scale is not None:
+            part = part * row_scale
+        for q in range(PLANE):
+            piece = part[q * prows : (q + 1) * prows]
+            part_f32[c, q] = piece
+            a_send[which, c, q] = piece.astype(bf16)
         for k in range(1, PLANE):
             a_copy(which, c, k).start()
 
@@ -376,37 +388,32 @@
             plane_peer(k),
         )
 
-    for i in range(CHUNKS):
-        w_copy(out_proj, w_sem, i).wait()
-    for c in range(CHUNKS):
-        stage_a(0, c, heads, None)
-    for i in range(CHUNKS):
-        w_copy(down_proj.at[0], d_sem, i).start()
-    for c in range(CHUNKS):
-        stage_b(0, c)
-    square = jnp.zeros((rows_dev, 1), f32)
-    for c in range(CHUNKS):
+    my_slot = my_q * planes + my_z
+
+    def stage_own(c, square):
         cols = slice(c * cc, (c + 1) * cc)
         value = hidden[:, cols].astype(f32) + stage_sum(0, c)
         residual[c] = value
-        square = square + jnp.sum(value * value, axis=1, keepdims=True)
         scaled = (value * gain[:, cols]).astype(bf16)
         own_rows[c] = scaled
         for k in range(1, planes):
             z_copy(c, k).start()
         z_recv[c, my_z] = scaled
-    inv_rms = lax.rsqrt(square * (1.0 / width) + norm_eps)
-    info_own[...] = jnp.where(lane == 127, inv_rms, info)
-    my_slot = my_q * planes + my_z
-
-    @pl.loop(1, n)
-    def _(k):
-        remote(
-            info_own, info_all.at[my_slot], i_ss.at[k], i_rs.at[k], lax.rem(me + k, n)
-        ).start()
-
-    info_all[my_slot] = info_own[...]
-    for c in range(CHUNKS):
+        return square + jnp.sum(value * value, axis=1, keepdims=True)
+
+    def send_info(square):
+        inv_rms = lax.rsqrt(square * (1.0 / width) + norm_eps)
+        info_own[...] = jnp.where(lane == 127, inv_rms, info)
+
+        @pl.loop(1, n)
+        def _(k):
+            remote(
+                info_own, info_all.at[my_slot], i_ss.at[k], i_rs.at[k], lax.rem(me + k, n)
+            ).start()
+
+        info_all[my_slot] = info_own[...]
+
+    def stage_spread(c):
         for k in range(1, planes):
             z_arrival(c, k).wait_recv()
         for z in range(planes):
@@ -417,24 +424,36 @@
             p_copy(c, k).start()
         p_recv[c, my_q] = block
 
-    for c in range(CHUNKS):
+    def stage_units(c):
         gu_copy(gate_proj, g_buf, 0, c).wait()
         gu_copy(up_proj, u_buf, 1, c).wait()
         for k in range(1, PLANE):
             p_arrival(c, k).wait_recv()
         x = jnp.concatenate([p_recv[c, q].astype(f32) for q in range(PLANE)], axis=0).astype(bf16)
-
-        @pl.loop(0, g_acc.shape[1] // TILE)
-        def _(t):
-            cols = pl.ds(pl.multiple_of(t * TILE, TILE), TILE)
-            span = slice(c * cc, (c + 1) * cc)
-            g = jnp.dot(x, g_buf[span, cols], preferred_element_type=f32)
-            u = jnp.dot(x, u_buf[span, cols], preferred_element_type=f32)
-            if c > 0:
-                g = g + g_acc[:, cols]
-                u = u + u_acc[:, cols]
-            g_acc[:, cols] = g
-            u_acc[:, cols] = u
+        span = slice(c * cc, (c + 1) * cc)
+        for acc, mat in ((g_acc, g_buf), (u_acc, u_buf)):
+            part = jnp.dot(x, mat[span, :], preferred_element_type=f32)
+            acc[...] = part if c == 0 else acc[...] + part
+
+    for i in range(LOADS):
+        w_copy(out_proj, w_sem, i).wait()
+    square = jnp.zeros((rows_dev, 1), f32)
+    for stage, c in step_order(chunks, (0.6, 2.4, 3.5, 3.5, 2.4)):
+        if stage == 0:
+            stage_a(0, c, heads, None)
+            if c == chunks - 1:
+                for i in range(LOADS):
+                    w_copy(down_proj.at[0], d_sem, i).start()
+        elif stage == 1:
+            stage_b(0, c)
+        elif stage == 2:
+            square = stage_own(c, square)
+            if c == chunks - 1:
+                send_info(square)
+        elif stage == 3:
+            stage_spread(c)
+        else:
+            stage_units(c)
 
     @pl.loop(1, n)
     def _(k):
@@ -450,14 +469,15 @@
     row_weight = jnp.sum(jnp.where(lane == me, info, 0.0), axis=1, keepdims=True)
     gate = g_acc[...] * row_inv
     units[...] = (gate / (1.0 + jnp.exp(-gate)) * (u_acc[...] * row_inv)).astype(bf16)
-    for i in range(CHUNKS):
+    for i in range(LOADS):
         w_copy(down_proj.at[0], d_sem, i).wait()
-    for c in range(CHUNKS):
-        stage_a(1, c, units, row_weight)
-    for c in range(CHUNKS):
-        stage_b(1, c)
-    for c in range(CHUNKS):
-        out[:, c * cc : (c + 1) * cc] = (residual[c] + stage_sum(1, c)).astype(bf16)
+    for stage, c in step_order(chunks, (0.6, 2.4, 3.5)):
+        if stage == 0:
+            stage_a(1, c, units, row_weight)
+        elif stage == 1:
+            stage_b(1, c)
+        else:
+            out[:, c * cc : (c + 1) * cc] = (residual[c] + stage_sum(1, c)).astype(bf16)
 
     for r in range(rows_dev):
 
@@ -474,7 +494,7 @@
             info_own, info_all.at[0], i_ss.at[k], i_rs.at[k], lax.rem(me + k, n)
         ).wait_send()
 
-    for c in range(CHUNKS):
+    for c in range(chunks):
         for which in range(2):
             for k in range(1, PLANE):
                 a_copy(which, c, k).wait_send()
@@ -502,11 +522,14 @@
 ):
     n = lax.axis_size("ep")
     planes = n // PLANE
+    queries = jnp.swapaxes(queries, 1, 2)
+    latent_cache = jnp.swapaxes(latent_cache, 1, 2)
     rows_dev, width = hidden.shape
     rows, prows = n * rows_dev, planes * rows_dev
     heads_dev, latent, vdim = value_up.shape
     ff = gate_proj.shape[2]
-    cc = width // CHUNKS
+    chunks = chunks_of(width)
+    cc = width // chunks
     bf16, f32 = jnp.bfloat16, jnp.float32
     vmem, anyspace = pl.BlockSpec(memory_space=pltpu.VMEM), pl.BlockSpec(memory_space=pl.ANY)
     dma = pltpu.SemaphoreType.DMA
@@ -539,18 +562,18 @@
             pltpu.VMEM((rows, heads_dev, latent), bf16),
             pltpu.VMEM((latent // 128, rows * heads_dev, 128), f32),
             pltpu.VMEM((rows, heads_dev * vdim), bf16),
-            pltpu.VMEM((CHUNKS, PLANE, prows, cc), f32),
-            pltpu.VMEM((2, CHUNKS, PLANE, prows, cc), bf16),
-            pltpu.VMEM((2, CHUNKS, PLANE - 1, prows, cc), bf16),
-            pltpu.VMEM((CHUNKS, planes, rows_dev, cc), f32),
-            pltpu.VMEM((2, CHUNKS, planes, rows_dev, cc), bf16),
-            pltpu.VMEM((2, CHUNKS, planes - 1, rows_dev, cc), bf16),
-            pltpu.VMEM((CHUNKS, rows_dev, cc), f32),
-            pltpu.VMEM((CHUNKS, rows_dev, cc), bf16),
-            pltpu.VMEM((CHUNKS, planes, rows_dev, cc), bf16),
-            pltpu.VMEM((CHUNKS, prows, cc), f32),
-            pltpu.VMEM((CHUNKS, prows, cc), bf16),
-            pltpu.VMEM((CHUNKS, PLANE, prows, cc), bf16),
+            pltpu.VMEM((chunks, PLANE, prows, cc), f32),
+            pltpu.VMEM((2, chunks, PLANE, prows, cc), bf16),
+            pltpu.VMEM((2, chunks, PLANE - 1, prows, cc), bf16),
+            pltpu.VMEM((chunks, planes, rows_dev, cc), f32),
+            pltpu.VMEM((2, chunks, planes, rows_dev, cc), bf16),
+            pltpu.VMEM((2, chunks, planes - 1, rows_dev, cc), bf16),
+            pltpu.VMEM((chunks, rows_dev, cc), f32),
+            pltpu.VMEM((chunks, rows_dev, cc), bf16),
+            pltpu.VMEM((chunks, planes, rows_dev, cc), bf16),
+            pltpu.VMEM((chunks, prows, cc), f32),
+            pltpu.VMEM((chunks, prows, cc), bf16),
+            pltpu.VMEM((chunks, PLANE, prows, cc), bf16),
             pltpu.VMEM((rows_dev, 128), f32),
             pltpu.VMEM((n, rows_dev, 128), f32),
             pltpu.VMEM((rows, 128), f32),
@@ -558,19 +581,19 @@
             pltpu.VMEM((rows, ff), f32),
             pltpu.VMEM((rows, ff), bf16),
             dma((2 + rows_dev,)),
-            dma((CHUNKS,)),
-            dma((2, CHUNKS)),
-            dma((CHUNKS,)),
+            dma((LOADS,)),
+            dma((2, chunks)),
+            dma((LOADS,)),
             dma((rows_dev, n)),
             dma((rows_dev, n)),
-            dma((2, CHUNKS, PLANE - 1)),
-            dma((2, CHUNKS, PLANE - 1)),
-            dma((2, CHUNKS, planes - 1)),
-            dma((2, CHUNKS, planes - 1)),
-            dma((CHUNKS, planes - 1)),
-            dma((CHUNKS, planes - 1)),
-            dma((CHUNKS, PLANE - 1)),
-            dma((CHUNKS, PLANE - 1)),
+            dma((2, chunks, PLANE - 1)),
+            dma((2, chunks, PLANE - 1)),
+            dma((2, chunks, planes - 1)),
+            dma((2, chunks, planes - 1)),
+            dma((chunks, planes - 1)),
+            dma((chunks, planes - 1)),
+            dma((chunks, PLANE - 1)),
+            dma((chunks, PLANE - 1)),
             dma((n,)),
             dma((n,)),
         ],

time: 71.2 us -> 51.5 us (0.72)
  Pallas kernels: 59.8 us -> 49.9 us
  local copies, waits for them, and re-layouts: 10.9 us -> 1.38 us
    pallas_call x1, Pallas kernels: 59.8 us -> 49.9 us  [fused_on_device(): pl.pallas_call(functools.partial(fused_kernel, n), out_shape=jax.ShapeDty...]
    unnamed x3 -> x1, local copies, waits for them, and re-layouts: 10.9 us -> 1.38 us
where the time goes in v2:
time: 51.5 us; the launch traced here: 51.2 us
  Pallas kernels  49.9 us (97%)
  local copies, waits for them, and re-layouts  1.38 us (3%)
    pallas_call x1, Pallas kernels, fused_on_device(): pl.pallas_call(functools.partial(fused_kernel, n), out_shape=jax.ShapeDty...  49.9 us
    unnamed x1, local copies, waits for them, and re-layouts  1.38 us

profile of v2, /device:TPU:0, one launch (start us, length us, event | category | flops | bytes accessed | tf_op | source)
XLA Modules:
  0.0 51.2 jit_solution(4581025344350758600)
XLA Ops:
  0.0 49.9 %fused_layer.1 = bf16[2,7168]{1,0:T(2,128)(2,1)} custom-call(bf16[2,7168]{1,0:T(2,128)(2,1)} %hidden.1, bf16[2,576,128]{2,1,0:T(8,128)(2,1)} %bitcast.4, bf16[2,576,2048]{2,1,0:T(8,128)(2,1)} %bitcast.3, s32[2]{0:T(128)} %lengths.1, bf16[8,512,128]{2,1,0:T(8,128)(2,1)} %value_up.1, bf16[1024,7168]{1,0:T(8,128)(2,1)} %out_proj.1, f32[1,7168]{1,0:T(1,128)} %bitcast.5, ...), custom_call_target="tpu_custom_call" | custom-call | tf_op jit(solution)/shard_map/fused_layer/pallas_call | solution.py:536
  49.9 1.4 %copy.14 = bf16[2,7168]{1,0:T(2,128)(2,1)} copy(bf16[2,7168]{1,0:T(2,128)(2,1)} %fused_layer.1) | data formatting | bytes 57344

commit v3 on v2

--- a/solution.py
+++ b/solution.py
@@ -135,19 +135,25 @@
 
 def fused_kernel(
     n,
-    hidden,
+    hidden_hbm,
     queries,
     cache,
-    lengths,
+    lengths_hbm,
     value_up,
     out_proj,
-    gain,
-    ids,
-    weights,
+    gain_hbm,
+    ids_hbm,
+    weights_hbm,
     gate_proj,
     up_proj,
     down_proj,
     out,
+    hidden,
+    gain,
+    ids,
+    weights,
+    lengths,
+    q_rows,
     q_buf,
     c_buf,
     vu_buf,
@@ -216,9 +222,21 @@
     for r in range(rows_dev):
         loads.append(pltpu.make_async_copy(cache.at[r], c_buf.at[r], load_sem.at[1 + r]))
     load_vu = pltpu.make_async_copy(value_up, vu_buf, load_sem.at[1 + rows_dev])
-    for copy in loads:
-        copy.start()
-    load_vu.start()
+    small = [
+        pltpu.make_async_copy(src, dst, load_sem.at[2 + rows_dev + i])
+        for i, (src, dst) in enumerate(
+            (
+                (lengths_hbm, lengths),
+                (ids_hbm, ids),
+                (weights_hbm, weights),
+                (hidden_hbm, hidden),
+                (gain_hbm, gain),
+            )
+        )
+    ]
+    small[0].start()
+    loads[0].start()
+    loads[1].start()
 
     barrier = pltpu.get_barrier_semaphore()
 
@@ -241,17 +259,14 @@
         span = pl.ds(i * cc, cc)
         return pltpu.make_async_copy(src.at[0, span, :], dst.at[span, :], gu_sem.at[j, i])
 
-    loads[0].wait()
-    for r in range(rows_dev):
-        loads[1 + r].wait()
-        if r == 0:
-            for i in range(LOADS):
-                w_copy(out_proj, w_sem, i).start()
+    half = n // 2
+    side = lax.div(me, half)
+    my_low = lax.rem(me, half)
+
+    def attend(r, where):
+        span = pl.ds(pl.multiple_of(where * half * heads_dev, half * heads_dev), half * heads_dev)
         scores = (
-            lax.dot_general(
-                q_buf[r], c_buf[r], (((0,), (0,)), ((), ())), preferred_element_type=f32
-            )
-            * score_scale
+            jnp.dot(q_rows[r, span, :], c_buf[r], preferred_element_type=f32) * score_scale
         )
         positions = lax.broadcasted_iota(jnp.int32, scores.shape, 1)
         scores = jnp.where(positions < lengths[r], scores, -jnp.inf)
@@ -265,20 +280,46 @@
             preferred_element_type=f32,
         )
         acc = acc / total
-        for d in range(n):
-            lat_send[r, d] = acc[d * heads_dev : (d + 1) * heads_dev].astype(bf16)
-        if r == 0:
-            pl.semaphore_wait(barrier, n - 1)
+        for i in range(half):
+            lat_send[r, where * half + i] = acc[i * heads_dev : (i + 1) * heads_dev].astype(bf16)
+
+    def send_latent(r, where, first):
         slot = my_q * prows + my_z * rows_dev + r
 
-        @pl.loop(1, n)
-        def _(k):
-            peer = lax.rem(me + k, n)
+        @pl.loop(first, half)
+        def _(i):
+            peer = where * half + lax.rem(my_low + i, half)
+            k = lax.rem(peer - me + n, n)
             remote(
                 lat_send.at[r, peer], lat_recv.at[slot], lat_ss.at[r, k], lat_rs.at[r, k], peer
             ).start()
 
-        lat_recv[slot] = lat_send[r, me]
+        if first:
+            lat_recv[slot] = lat_send[r, me]
+
+    loads[0].wait()
+    for r in range(rows_dev):
+        q_rows[r] = q_buf[r].T
+    small[0].wait()
+    for r in range(rows_dev):
+        loads[1 + r].wait()
+        if r + 1 < rows_dev:
+            loads[2 + r].start()
+        if r == 0:
+            load_vu.start()
+            for copy in small[1:]:
+                copy.start()
+            for i in range(LOADS):
+                w_copy(out_proj, w_sem, i).start()
+        attend(r, 1 - side)
+        if r == 0:
+            pl.semaphore_wait(barrier, n - 1)
+        send_latent(r, 1 - side, 0)
+    for r in range(rows_dev):
+        attend(r, side)
+        send_latent(r, side, 1)
+    for copy in small[1:]:
+        copy.wait()
 
     lane = lax.broadcasted_iota(jnp.int32, (rows_dev, 128), 1)
     info = jnp.zeros((rows_dev, 128), f32)
@@ -469,41 +510,43 @@
     row_weight = jnp.sum(jnp.where(lane == me, info, 0.0), axis=1, keepdims=True)
     gate = g_acc[...] * row_inv
     units[...] = (gate / (1.0 + jnp.exp(-gate)) * (u_acc[...] * row_inv)).astype(bf16)
+    def drain(which, c):
+        for k in range(1, PLANE):
+            a_copy(which, c, k).wait_send()
+        for k in range(1, planes):
+            b_copy(which, c, k).wait_send()
+
+    def drain_first():
+        @pl.loop(1, n)
+        def _(k):
+            peer = lax.rem(me + k, n)
+            for r in range(rows_dev):
+                remote(
+                    lat_send.at[r, peer], lat_recv.at[0], lat_ss.at[r, k], lat_rs.at[r, k], peer
+                ).wait_send()
+            remote(info_own, info_all.at[0], i_ss.at[k], i_rs.at[k], peer).wait_send()
+
+        for c in range(chunks):
+            drain(0, c)
+            for k in range(1, planes):
+                z_copy(c, k).wait_send()
+            for k in range(1, PLANE):
+                p_copy(c, k).wait_send()
+
     for i in range(LOADS):
         w_copy(down_proj.at[0], d_sem, i).wait()
     for stage, c in step_order(chunks, (0.6, 2.4, 3.5)):
         if stage == 0:
             stage_a(1, c, units, row_weight)
+            if c == chunks - 1:
+                drain_first()
         elif stage == 1:
             stage_b(1, c)
         else:
             out[:, c * cc : (c + 1) * cc] = (residual[c] + stage_sum(1, c)).astype(bf16)
 
-    for r in range(rows_dev):
-
-        @pl.loop(1, n)
-        def _(k):
-            peer = lax.rem(me + k, n)
-            remote(
-                lat_send.at[r, peer], lat_recv.at[0], lat_ss.at[r, k], lat_rs.at[r, k], peer
-            ).wait_send()
-
-    @pl.loop(1, n)
-    def _(k):
-        remote(
-            info_own, info_all.at[0], i_ss.at[k], i_rs.at[k], lax.rem(me + k, n)
-        ).wait_send()
-
     for c in range(chunks):
-        for which in range(2):
-            for k in range(1, PLANE):
-                a_copy(which, c, k).wait_send()
-            for k in range(1, planes):
-                b_copy(which, c, k).wait_send()
-        for k in range(1, planes):
-            z_copy(c, k).wait_send()
-        for k in range(1, PLANE):
-            p_copy(c, k).wait_send()
+        drain(1, c)
 
 
 def fused_on_device(
@@ -536,22 +579,15 @@
     return pl.pallas_call(
         functools.partial(fused_kernel, n),
         out_shape=jax.ShapeDtypeStruct(hidden.shape, bf16),
-        in_specs=[
-            vmem,
-            anyspace,
-            anyspace,
-            pl.BlockSpec(memory_space=pltpu.SMEM),
-            anyspace,
-            anyspace,
-            vmem,
-            vmem,
-            vmem,
-            anyspace,
-            anyspace,
-            anyspace,
-        ],
+        in_specs=[anyspace] * 12,
         out_specs=vmem,
         scratch_shapes=[
+            pltpu.VMEM(hidden.shape, bf16),
+            pltpu.VMEM((1, width), f32),
+            pltpu.VMEM(expert_ids.shape, jnp.int32),
+            pltpu.VMEM(gate_weights.shape, f32),
+            pltpu.SMEM(cache_lengths.shape, jnp.int32),
+            pltpu.VMEM((rows_dev, queries.shape[2], queries.shape[1]), bf16),
             pltpu.VMEM(queries.shape, bf16),
             pltpu.VMEM(latent_cache.shape, bf16),
             pltpu.VMEM(value_up.shape, bf16),
@@ -580,7 +616,7 @@
             pltpu.VMEM((rows, ff), f32),
             pltpu.VMEM((rows, ff), f32),
             pltpu.VMEM((rows, ff), bf16),
-            dma((2 + rows_dev,)),
+            dma((7 + rows_dev,)),
             dma((LOADS,)),
             dma((2, chunks)),
             dma((LOADS,)),

time: 51.5 us -> 50.5 us (0.981)
  Pallas kernels: 49.9 us -> 49 us
    pallas_call x1, Pallas kernels: 49.9 us -> 49 us  [fused_on_device(): pl.pallas_call(functools.partial(fused_kernel, n), out_shape=jax.ShapeDty...]
where the time goes in v3:
time: 50.5 us; the launch traced here: 50.3 us
  Pallas kernels  49 us (97%)
  local copies, waits for them, and re-layouts  1.38 us (3%)
    pallas_call x1, Pallas kernels, fused_on_device(): pl.pallas_call(functools.partial(fused_kernel, n), out_shape=jax.ShapeDty...  49 us
    unnamed x1, local copies, waits for them, and re-layouts  1.38 us

profile of v3, /device:TPU:0, one launch (start us, length us, event | category | flops | bytes accessed | tf_op | source)
XLA Modules:
  0.0 50.3 jit_solution(6972606315922317062)
XLA Ops:
  0.0 49.0 %fused_layer.1 = bf16[2,7168]{1,0:T(2,128)(2,1)} custom-call(bf16[2,7168]{1,0:T(2,128)(2,1)} %hidden_hbm.1, bf16[2,576,128]{2,1,0:T(8,128)(2,1)} %bitcast.4, bf16[2,576,2048]{2,1,0:T(8,128)(2,1)} %bitcast.3, s32[2]{0:T(128)} %lengths_hbm.1, bf16[8,512,128]{2,1,0:T(8,128)(2,1)} %value_up.1, bf16[1024,7168]{1,0:T(8,128)(2,1)} %out_proj.1, f32[1,7168]{1,0:T(1,128)} %bitcast.5, ...), custom_call_target="tpu_custom_call" | custom-call | tf_op jit(solution)/shard_map/fused_layer/pallas_call | solution.py:579
  49.0 1.4 %copy.14 = bf16[2,7168]{1,0:T(2,128)(2,1)} copy(bf16[2,7168]{1,0:T(2,128)(2,1)} %fused_layer.1) | data formatting | bytes 57344
